TPU v7x, 1024 devices: a whole 4x4x32 slice. The times are simulated.
1024 devices in a mesh: ctx: 16 (over z_lo), exp: 32 (over y, x, core), tp: 2 (over z_hi).
Axes of the slice: x: 4, y: 4, z: 32 (z_hi: 2, z_lo: 16; z = z_hi * 16 + z_lo), core: 2. Of those that a mesh axis runs over, the one named last changes fastest.
Arguments:
- queries: bfloat16 [512, 2, 4, 64, 128], P('ctx', 'tp', None, 'exp'), may hold values from -6 to 6
- keys: bfloat16 [4096, 4, 128], P('ctx'), may hold values from -6 to 6
- values: bfloat16 [4096, 4, 128], P('ctx'), may hold values from -6 to 6
- out_weight: bfloat16 [8192, 4096], P('exp'), may hold values from -0.0625 to 0.0625
- norm_gain: float32 [4096], replicated, may hold values from 0.5 to 1.5
- routes: int32 [4096, 8], P(('ctx', 'exp', 'tp')), may hold values from 0 to 127, as said below
- route_weight: float32 [4096, 8], P(('ctx', 'exp', 'tp')), may hold values from 0.05 to 1
- w_gate: bfloat16 [32, 4096, 384], P('exp', None, 'tp'), may hold values from -0.09375 to 0.09375
- w_up: bfloat16 [32, 4096, 384], P('exp', None, 'tp'), may hold values from -0.09375 to 0.09375
- w_down: bfloat16 [32, 384, 4096], P('exp', 'tp'), may hold values from -0.21875 to 0.21875
Outputs:
- layer_out: bfloat16 [4096, 4096], P(('ctx', 'exp', 'tp'))
Inputs may be any that keep to these rules, and one draw needn't show every extreme that they name: `routes`: each row names 8 different experts. In each aligned block of 4 rows no expert is named by more than 2 rows, and some expert is named by exactly 2 rows.
All inputs are finite; a program needn't handle non-finite values.
Results may differ from a plain program's by a relative error of at most 0.025.
Values may be sent and summed in bfloat16 or wider, within the bound.
A program may use at most 32 MiB of HBM per device.

v0:
```python
import jax
import jax.numpy as jnp
from jax import lax
from jax.sharding import PartitionSpec as P

CAP = 2


def in_one_piece(arrays, axis, dim, along):
    widths = [a.shape[along] for a in arrays]
    both = jnp.concatenate(arrays, axis=along)
    out = lax.all_gather(both, axis, axis=dim, tiled=True)
    return tuple(jnp.split(out, [sum(widths[:k]) for k in range(1, len(widths))], axis=along))


def split_up(shard, dim, length):
    before, after = (shard.shape[:dim], shard.shape[dim + 1 :])
    return jnp.moveaxis(shard.reshape(*before, length, -1, *after), dim, 0)


def sum_at_owner(shard, axis, dim):
    length = lax.axis_size(axis)
    pieces = lax.all_to_all(split_up(shard, dim, length), axis, 0, 0, tiled=True)
    return jnp.sum(pieces.astype(jnp.float32), axis=0)


def silu_mul(gate, up):
    return gate / (1.0 + jnp.exp(-gate)) * up


def on_device(
    queries, keys, values, out_weight, norm_gain, routes, route_weight, w_gate, w_up, w_down
):
    blocks, lanes, rows, local_heads, head_dim = queries.shape
    width = out_weight.shape[1]
    n_exp = lax.axis_size("exp")
    n_tp = lax.axis_size("tp")
    live_count = n_exp // 2
    ctx_index = lax.axis_index("ctx")
    exp_index = lax.axis_index("exp")
    tp_index = lax.axis_index("tp")
    group = local_heads * n_exp // keys.shape[1]
    kv_head = exp_index * local_heads // group
    key_mine = lax.dynamic_index_in_dim(keys, kv_head, 1, keepdims=False)
    value_mine = lax.dynamic_index_in_dim(values, kv_head, 1, keepdims=False)
    query_rows = blocks * rows
    query_vector = queries.reshape(query_rows, local_heads, head_dim).transpose(1, 0, 2)
    block_ids = jnp.arange(blocks, dtype=jnp.int32)[:, None]
    inner = jnp.arange(rows, dtype=jnp.int32)[None, :]
    query_pos = (((ctx_index * blocks + block_ids) * n_tp + tp_index) * rows + inner).reshape(-1)
    score_scale = head_dim ** (-0.5)
    highest = jnp.full((local_heads, query_rows), -1e30, jnp.float32)
    key_portion, value_portion = in_one_piece((key_mine, value_mine), "ctx", 0, 1)
    logit_score = (
        jnp.einsum("qbr,zr->qbz", query_vector, key_portion, preferred_element_type=jnp.float32)
        * score_scale
    )
    key_pos = jnp.arange(key_portion.shape[0], dtype=jnp.int32)
    allowed = (key_pos[None, :] <= query_pos[:, None])[None, :, :]
    logit_score = jnp.where(allowed, logit_score, -1e30)
    new_high = jnp.maximum(highest, jnp.max(logit_score, axis=2))
    attention_probability = jnp.where(allowed, jnp.exp(logit_score - new_high[:, :, None]), 0.0)
    total = jnp.sum(attention_probability, axis=2)
    accum = jnp.einsum(
        "axt,ty->axy",
        attention_probability.astype(jnp.bfloat16),
        value_portion,
        preferred_element_type=jnp.float32,
    )
    highest, total, accum = (new_high, total, accum)
    mixed = (accum / total[:, :, None]).astype(jnp.bfloat16)
    mixed_rows = mixed.transpose(1, 0, 2).reshape(query_rows, local_heads * head_dim)
    summed = sum_at_owner(
        jnp.dot(mixed_rows, out_weight, preferred_element_type=jnp.float32).astype(jnp.bfloat16),
        "exp",
        0,
    )
    state = summed.astype(jnp.bfloat16)
    state_wide = state.astype(jnp.float32)
    inverse = lax.rsqrt(jnp.mean(state_wide * state_wide, axis=1, keepdims=True) + 1e-06)
    normed = (state_wide * inverse * norm_gain[None, :]).astype(jnp.bfloat16)
    picks = routes.shape[1]
    flat = routes.reshape(-1)
    order = jnp.arange(flat.shape[0], dtype=jnp.int32)
    same = (flat[:, None] == flat[None, :]) & (order[None, :] < order[:, None])
    slot = jnp.sum(same.astype(jnp.int32), axis=1)
    target = jnp.where(flat < live_count, flat * CAP + slot, -1)
    slots = jnp.arange(live_count * CAP, dtype=jnp.int32)
    hit = (
        (target[None, :] == slots[:, None])
        .astype(jnp.float32)
        .reshape(live_count * CAP, rows, picks)
    )
    pick = jnp.sum(hit, axis=2).astype(jnp.bfloat16)
    buffer = (
        jnp.dot(pick, normed, preferred_element_type=jnp.float32)
        .astype(jnp.bfloat16)
        .reshape(live_count, CAP, width)
    )
    share = route_weight / jnp.sum(route_weight, axis=1, keepdims=True)
    mix = jnp.sum(hit * share[None, :, :], axis=2).T
    outgoing = jnp.broadcast_to(buffer[None, :, None], (2, live_count, n_tp, CAP, width)).reshape(
        n_exp * n_tp, CAP, width
    )
    received = lax.all_to_all(outgoing, ("exp", "tp"), split_axis=0, concat_axis=0, tiled=True)
    flat_rows = received.reshape(-1, width)
    gate = jnp.dot(flat_rows, w_gate[0], preferred_element_type=jnp.float32)
    up = jnp.dot(flat_rows, w_up[0], preferred_element_type=jnp.float32)
    hidden = silu_mul(gate, up).astype(jnp.bfloat16)
    result = jnp.dot(hidden, w_down[0], preferred_element_type=jnp.float32).astype(jnp.bfloat16)
    returned = lax.all_to_all(
        result.reshape(received.shape), ("exp", "tp"), split_axis=0, concat_axis=0, tiled=True
    )
    expert_output_rows = jnp.sum(
        returned.astype(jnp.float32).reshape(2, live_count, n_tp, CAP, width), axis=(0, 2)
    )
    moe = jnp.dot(
        mix, expert_output_rows.reshape(live_count * CAP, width), preferred_element_type=jnp.float32
    )
    return (state_wide + moe).astype(jnp.bfloat16)


def solution(mesh):
    in_specs = (
        P("ctx", "tp", None, "exp", None),
        P("ctx", None, None),
        P("ctx", None, None),
        P("exp", None),
        P(),
        P(("ctx", "exp", "tp"), None),
        P(("ctx", "exp", "tp"), None),
        P("exp", None, "tp"),
        P("exp", None, "tp"),
        P("exp", "tp", None),
    )
    out_specs = P(("ctx", "exp", "tp"), None)
    return jax.shard_map(
        on_device, mesh=mesh, in_specs=in_specs, out_specs=out_specs, check_vma=False
    )
```

profile of v0, /device:TPU:97, one launch (start us, length us, event | category | flops | bytes accessed | tf_op | source)
XLA Modules:
  0.0 437.9 jit_solution(1834121226558000908)
XLA Ops:
  6.5 0.0 copy-start
  6.5 0.0 all-gather.2.cloned.1.call-start
  6.5 1.5 constant_dynamic-slice_fusion
  8.0 0.7 pad_maximum_fusion
  8.7 0.0 all-gather.2.cloned.1.call-update
  8.7 0.1 iota_add_fusion
  8.8 0.1 add.79
  8.9 0.3 iota_compare_fusion
  9.3 166.1 %all-gather.2.cloned.1.call-done = bf16[4096,256]{1,0:T(8,128)(2,1)} async-done(((bf16[256,256]{1,0:T(8,128)(2,1)}), bf16[4096,256]{1,0:T(8,128)(2,1)}) %all-gather.2.cloned.1.call-update) | async-done | bytes 2097168 | tf_op jit(solution)/shard_map/all_gather | solution.py:12
  175.4 2.1 fusion.49
  177.5 0.0 copy-start.4
  177.5 0.8 fusion.3
  178.3 0.7 copy-done.4
  179.1 1.0 fusion.29
  180.1 0.0 copy-done
  180.1 0.5 convolution_convert_fusion.1
  180.6 0.0 copy-start.2
  180.6 0.0 copy-start.3
  180.6 1.2 reshape.113
  181.8 0.0 copy-start.1
  181.8 21.1 %all-to-all-start = ((bf16[32,4,4096]{2,1,0:T(4,128)(2,1)}), bf16[32,4,4096]{2,1,0:T(4,128)(2,1)S(1)}, u32[]{:S(2)}, u32[]{:S(2)}) async-start(bf16[32,4,4096]{2,1,0:T(4,128)(2,1)} %reshape.113), calls=%async_computation | async-start | bytes 2097152 | tf_op jit(solution)/shard_map/all_to_all | solution.py:23
  202.9 0.0 copy-done.2
  202.9 0.1 eq.13
  203.0 0.2 convert_reduce_fusion.2
  203.2 0.1 reduce_sum.80
  203.3 0.0 copy-done.3
  203.3 0.1 reduce_sum.81
  203.4 0.1 broadcast_divide_fusion
  203.5 0.1 convert_reduce_fusion.1
  203.6 16.4 %all-to-all-done = bf16[32,4,4096]{2,1,0:T(4,128)(2,1)S(1)} async-done(((bf16[32,4,4096]{2,1,0:T(4,128)(2,1)}), bf16[32,4,4096]{2,1,0:T(4,128)(2,1)S(1)}, u32[]{:S(2)}, u32[]{:S(2)}) %all-to-all-start) | async-done | bytes 1048608 | tf_op jit(solution)/shard_map/all_to_all | solution.py:23
  219.9 0.4 reduce_sum.78
  220.4 0.1 fusion.36
  220.5 0.0 copy-done.1
  220.5 0.3 convolution_convert_fusion.2
  220.8 0.2 broadcast_in_dim.51
  221.0 1.0 broadcast_in_dim.52
  222.0 137.3 %all_to_all.15 = bf16[64,2,4096]{2,1,0:T(2,128)(2,1)} all-to-all(bf16[64,2,4096]{2,1,0:T(2,128)(2,1)S(1)} %bitcast.57), channel_id=1, replica_groups=mesh['ctx'=16,'exp'=32,'tp'=2] {'exp','tp'}, dimensions={0} | all-to-all | bytes 2097152 | tf_op jit(solution)/shard_map/all_to_all | solution.py:105
  359.3 1.5 reshape.115
  360.8 2.0 fusion.13
  362.8 4.4 %convolution_convert_fusion = bf16[128,4096]{1,0:T(8,128)(2,1)} fusion(bf16[1,192,4096]{2,1,0:T(8,128)(2,1)} %param.19, bf16[128,4096]{1,0:T(8,128)(2,1)S(1)} %reshape.115, bf16[1,4096,192]{1,2,0:T(8,128)(2,1)} %param.18, f32[128,192]{0,1:T(8,128)S(1)} %fusion.13), kind=kOutput, calls=%fused_computation.3 | convolution fusion | flops 403300352 | bytes 5341184 | tf_op jit(solution)/shard_map/dot_general | solution.py:110
  367.2 1.7 reshape.116
  369.0 60.0 %all_to_all.16 = bf16[64,2,4096]{2,1,0:T(2,128)(2,1)S(1)} all-to-all(bf16[64,2,4096]{2,1,0:T(2,128)(2,1)S(1)} %reshape.116), channel_id=1, replica_groups=mesh['ctx'=16,'exp'=32,'tp'=2] {'exp','tp'}, dimensions={0} | all-to-all | bytes 2097152 | tf_op jit(solution)/shard_map/all_to_all | solution.py:111
  429.0 1.2 convert_reduce_fusion
  430.2 0.1 reshape.119
  430.3 0.8 fusion.2
  (6 shorter events, 0.0 us)
Async XLA Ops:
  6.5 173.5 %copy-start = (bf16[256,4096]{1,0:T(8,128)(2,1)S(1)}, bf16[256,4096]{1,0:T(8,128)(2,1)}, u32[]{:S(2)}) copy-start(bf16[256,4096]{1,0:T(8,128)(2,1)} %param.13) | copy-start | bytes 6291460
  6.5 168.8 %all-gather.2.cloned.1.call-start = ((), (), s32[]{:S(2)}) async-start(), calls=%async_computation.3 | async-start | bytes 2228224 | tf_op jit(solution)/shard_map/all_gather | solution.py:12
  177.5 1.6 copy-start.4
  180.6 22.3 %copy-start.2 = (s32[4,8]{1,0:T(4,128)S(1)}, s32[4,8]{1,0:T(4,128)}, u32[]{:S(2)}) copy-start(s32[4,8]{1,0:T(4,128)} %param.15) | copy-start | bytes 388
  180.6 22.7 %copy-start.3 = (f32[4,8]{1,0:T(4,128)S(1)}, f32[4,8]{1,0:T(4,128)}, u32[]{:S(2)}) copy-start(f32[4,8]{1,0:T(4,128)} %param.16) | copy-start | bytes 388
  181.8 38.7 %copy-start.1 = (f32[4096]{0:T(1024)S(1)}, f32[4096]{0:T(1024)}, u32[]{:S(2)}) copy-start(f32[4096]{0:T(1024)} %param.14) | copy-start | bytes 49156
  181.8 38.1 %all-to-all-start = ((bf16[32,4,4096]{2,1,0:T(4,128)(2,1)}), bf16[32,4,4096]{2,1,0:T(4,128)(2,1)S(1)}, u32[]{:S(2)}, u32[]{:S(2)}) async-start(bf16[32,4,4096]{2,1,0:T(4,128)(2,1)} %reshape.113), calls=%async_computation | async-start | bytes 2097152 | tf_op jit(solution)/shard_map/all_to_all | solution.py:23
Sparse Core Ops, SparseCore 0:
  10.0 165.3 all-gather.1
where the time goes:
time: 438 us
  blocking collectives  197 us (45%)
  waiting for transfers between devices  182 us (42%)
  starting transfers between devices  21.1 us (5%)
  between operations  13.6 us (3%)
  matrix products  11 us (3%)
  local copies, waits for them, and re-layouts  8.22 us (2%)
    all_gather x1, waiting for transfers between devices, in_one_piece(): out = lax.all_gather(both, axis, axis=dim, tiled=True)  166 us
    all_to_all x1, blocking collectives, on_device(): lax.all_to_all(outgoing, ('exp', 'tp'), split_axis=0, concat_axis=0, tile...  137 us
    all_to_all x1, blocking collectives, on_device(): lax.all_to_all(result.reshape(received.shape), ('exp', 'tp'), split_axis=...  60 us
    all_to_all x1, starting transfers between devices, sum_at_owner(): lax.all_to_all(split_up(shard, dim, length), axis, 0, 0, tiled=True)  21.1 us
    all_to_all x1, waiting for transfers between devices, sum_at_owner(): lax.all_to_all(split_up(shard, dim, length), axis, 0, 0, tiled=True)  16.4 us
  transfers between devices with their start and end apart: 2, of which 2 were waited for; matrix products, arithmetic and copies ran while one was open for 0% of the time, Pallas kernels for 0%

commit v1 on v0

--- a/solution.py
+++ b/solution.py
@@ -1,16 +1,173 @@
+import functools
 import jax
 import jax.numpy as jnp
 from jax import lax
+from jax.experimental import pallas as pl
+from jax.experimental.pallas import tpu as pltpu
 from jax.sharding import PartitionSpec as P
 
+MESH = pl.DeviceIdType.MESH
+VMEM = pltpu.VMEM
+F32 = jnp.float32
+BF16 = jnp.bfloat16
+CHUNK = 256
+HALF = 128
+NC = 16
+
+
+def where_am_i():
+    c = lax.axis_index("ctx")
+    e = lax.axis_index("exp")
+    t = lax.axis_index("tp")
+    return t * NC + c, e // 8, lax.rem(e // 2, 4), lax.rem(e, 2)
+
+
+def device(z, y, x, k):
+    z = lax.rem(z + 2 * NC, 2 * NC)
+    y = lax.rem(y + 4, 4)
+    x = lax.rem(x + 4, 4)
+    return (lax.rem(z, NC), (y * 4 + x) * 2 + k, z // NC)
+
+
+def greet(devices):
+    barrier = pltpu.get_barrier_semaphore()
+    for d in devices:
+        pl.semaphore_signal(barrier, inc=1, device_id=d, device_id_type=MESH)
+    pl.semaphore_wait(barrier, len(devices))
+
+
+def remote(src, dst, ssem, rsem, dev):
+    return pltpu.make_async_remote_copy(
+        src_ref=src, dst_ref=dst, send_sem=ssem, recv_sem=rsem, device_id=dev, device_id_type=MESH
+    )
+
+
+def attention_kernel(q_ref, mine_ref, o_ref, kv, up_s, up_r, dn_s, dn_r, x_s, x_r, c_s, c_r):
+    z, y, x, k = where_am_i()
+    c = lax.axis_index("ctx")
+    t = lax.axis_index("tp")
+    half = lax.rem(x, 2)
+    up1, up2 = device(z + 1, y, x, k), device(z + 2, y, x, k)
+    dn1, dn2 = device(z - 1, y, x, k), device(z - 2, y, x, k)
+    beside = device(z, y, x + 1 - 2 * half, k)
+    other = device(z, y, x, 1 - k)
+    greet([up1, up2, dn1, dn2, beside, other])
+
+    own = mine_ref.at[k, pl.ds(half * HALF, HALF)]
+
+    def piece(pos):
+        return kv.at[k, pos, half]
+
+    def up_copy(p, src, dev):
+        return remote(src, piece(2 * p), up_s.at[p], up_r.at[p], dev)
+
+    def dn_copy(p, src, dev):
+        return remote(src, piece(2 * p + 1), dn_s.at[p], dn_r.at[p], dev)
+
+    def width(p):
+        return 2 if p < 7 else 1
+
+    def x_copy(p):
+        blk = kv.at[k, pl.ds(2 * p, width(p)), half]
+        return remote(blk, blk, x_s.at[p], x_r.at[p], beside)
+
+    def c_copy(p):
+        blk = kv.at[k, pl.ds(2 * p, width(p))]
+        return remote(blk, blk, c_s.at[p], c_r.at[p], other)
+
+    ups = [up_copy(0, own, up1), up_copy(1, own, up2)]
+    dns = [dn_copy(0, own, dn1), dn_copy(1, own, dn2)]
+    for p in range(2, 8):
+        ups.append(up_copy(p, piece(2 * p - 4), up2))
+    for p in range(2, 7):
+        dns.append(dn_copy(p, piece(2 * p - 3), dn2))
+    xs = [x_copy(p) for p in range(8)]
+    cs = [c_copy(p) for p in range(8)]
+    ups[0].start()
+    dns[0].start()
+    ups[1].start()
+    dns[1].start()
+
+    scale = 128 ** (-0.5)
+    q = q_ref[...].reshape(256, 128)
+
+    def scores(keys):
+        return lax.dot_general(q, keys, (((1,), (1,)), ((), ())), preferred_element_type=F32) * scale
+
+    def mix(prob, vals):
+        return jnp.dot(prob.astype(BF16), vals, preferred_element_type=F32)
+
+    s = scores(mine_ref[0])
+    row = lax.broadcasted_iota(jnp.int32, (256, CHUNK), 0) & 127
+    col = lax.broadcasted_iota(jnp.int32, (256, CHUNK), 1)
+    pos = ((row >> 2) * 2 + t) * 4 + (row & 3)
+    ok = col <= pos
+    s = jnp.where(ok, s, -1e30)
+    m = jnp.max(s, axis=1, keepdims=True)
+    e = jnp.where(ok, jnp.exp(s - m), 0.0)
+    l = jnp.sum(e, axis=1, keepdims=True)
+    acc = mix(e, mine_ref[1])
+
+    def z_stage(p):
+        ups[p].wait_recv()
+        if p + 2 < 8:
+            ups[p + 2].start()
+        if p < 7:
+            dns[p].wait_recv()
+            if p + 2 < 7:
+                dns[p + 2].start()
+        xs[p].start()
+
+    def x_stage(p):
+        xs[p].wait_recv()
+        cs[p].start()
+
+    def absorb(p, m, l, acc):
+        cs[p].wait_recv()
+        n = width(p)
+        keys = kv[0, pl.ds(2 * p, n)].reshape(n * CHUNK, 128)
+        vals = kv[1, pl.ds(2 * p, n)].reshape(n * CHUNK, 128)
+        off = p + 1
+        seen_up = c >= off
+        seen_dn = c + off >= NC
+        s = scores(keys)
+        lane = lax.broadcasted_iota(jnp.int32, (1, n * CHUNK), 1)
+        bias_up = jnp.where(seen_up, 0.0, -1e30)
+        bias_dn = jnp.where(seen_dn, 0.0, -1e30)
+        s = s + jnp.where(lane < CHUNK, bias_up, bias_dn)
+        m_new = jnp.maximum(m, jnp.max(s, axis=1, keepdims=True))
+        fade = jnp.exp(m - m_new)
+        e = jnp.exp(s - m_new)
+        return m_new, l * fade + jnp.sum(e, axis=1, keepdims=True), acc * fade + mix(e, vals)
+
+    for i in range(8 + 2):
+        if i < 8:
+            z_stage(i)
+        if 0 <= i - 1 < 8:
+            x_stage(i - 1)
+        if 0 <= i - 2 < 8:
+            m, l, acc = absorb(i - 2, m, l, acc)
+    out = (acc / l).astype(BF16)
+    o_ref[:, 0:128] = out[0:128]
+    o_ref[:, 128:256] = out[128:256]
+    for cp in ups + dns + xs + cs:
+        cp.wait_send()
+
+
+def attention(q, mine):
+    dma = pltpu.SemaphoreType.DMA
+    return pl.pallas_call(
+        attention_kernel,
+        out_shape=jax.ShapeDtypeStruct((128, 256), BF16),
+        in_specs=[pl.BlockSpec(memory_space=VMEM)] * 2,
+        out_specs=pl.BlockSpec(memory_space=VMEM),
+        scratch_shapes=[VMEM((2, 16, 2, HALF, 128), BF16)] + [dma((8,))] * 8,
+        compiler_params=pltpu.CompilerParams(collective_id=0, has_side_effects=True),
+        name="gather_attend",
+    )(q, mine)
+
+
 CAP = 2
-
-
-def in_one_piece(arrays, axis, dim, along):
-    widths = [a.shape[along] for a in arrays]
-    both = jnp.concatenate(arrays, axis=along)
-    out = lax.all_gather(both, axis, axis=dim, tiled=True)
-    return tuple(jnp.split(out, [sum(widths[:k]) for k in range(1, len(widths))], axis=along))
 
 
 def split_up(shard, dim, length):
@@ -41,35 +198,15 @@
     tp_index = lax.axis_index("tp")
     group = local_heads * n_exp // keys.shape[1]
     kv_head = exp_index * local_heads // group
-    key_mine = lax.dynamic_index_in_dim(keys, kv_head, 1, keepdims=False)
-    value_mine = lax.dynamic_index_in_dim(values, kv_head, 1, keepdims=False)
+    mine = jnp.stack(
+        [
+            lax.dynamic_index_in_dim(keys, kv_head, 1, keepdims=False),
+            lax.dynamic_index_in_dim(values, kv_head, 1, keepdims=False),
+        ]
+    )
     query_rows = blocks * rows
     query_vector = queries.reshape(query_rows, local_heads, head_dim).transpose(1, 0, 2)
-    block_ids = jnp.arange(blocks, dtype=jnp.int32)[:, None]
-    inner = jnp.arange(rows, dtype=jnp.int32)[None, :]
-    query_pos = (((ctx_index * blocks + block_ids) * n_tp + tp_index) * rows + inner).reshape(-1)
-    score_scale = head_dim ** (-0.5)
-    highest = jnp.full((local_heads, query_rows), -1e30, jnp.float32)
-    key_portion, value_portion = in_one_piece((key_mine, value_mine), "ctx", 0, 1)
-    logit_score = (
-        jnp.einsum("qbr,zr->qbz", query_vector, key_portion, preferred_element_type=jnp.float32)
-        * score_scale
-    )
-    key_pos = jnp.arange(key_portion.shape[0], dtype=jnp.int32)
-    allowed = (key_pos[None, :] <= query_pos[:, None])[None, :, :]
-    logit_score = jnp.where(allowed, logit_score, -1e30)
-    new_high = jnp.maximum(highest, jnp.max(logit_score, axis=2))
-    attention_probability = jnp.where(allowed, jnp.exp(logit_score - new_high[:, :, None]), 0.0)
-    total = jnp.sum(attention_probability, axis=2)
-    accum = jnp.einsum(
-        "axt,ty->axy",
-        attention_probability.astype(jnp.bfloat16),
-        value_portion,
-        preferred_element_type=jnp.float32,
-    )
-    highest, total, accum = (new_high, total, accum)
-    mixed = (accum / total[:, :, None]).astype(jnp.bfloat16)
-    mixed_rows = mixed.transpose(1, 0, 2).reshape(query_rows, local_heads * head_dim)
+    mixed_rows = attention(query_vector, mine)
     summed = sum_at_owner(
         jnp.dot(mixed_rows, out_weight, preferred_element_type=jnp.float32).astype(jnp.bfloat16),
         "exp",

time: 438 us -> 297 us (0.68)
  the two profiles are of different devices: /device:TPU:97 before, /device:TPU:33 now
where the time goes in v1:
time: 297 us
  blocking collectives  211 us (71%)
  Pallas kernels  42.4 us (14%)
  waiting for transfers between devices  16.4 us (6%)
  local copies, waits for them, and re-layouts  8.85 us (3%)
  matrix products  8.72 us (3%)
  starting transfers between devices  6.66 us (2%)
    all_to_all x1, blocking collectives, on_device(): lax.all_to_all(outgoing, ('exp', 'tp'), split_axis=0, concat_axis=0, tile...  131 us
    all_to_all x1, blocking collectives, on_device(): lax.all_to_all(result.reshape(received.shape), ('exp', 'tp'), split_axis=...  80.1 us
    pallas_call x1, Pallas kernels, attention(): pl.pallas_call(attention_kernel, out_shape=jax.ShapeDtypeStruct((128, 256...  42.4 us
    all_to_all x1, waiting for transfers between devices, sum_at_owner(): lax.all_to_all(split_up(shard, dim, length), axis, 0, 0, tiled=True)  16.4 us
    all_to_all x1, starting transfers between devices, sum_at_owner(): lax.all_to_all(split_up(shard, dim, length), axis, 0, 0, tiled=True)  6.66 us
  transfers between devices with their start and end apart: 1, of which 1 were waited for; matrix products, arithmetic and copies ran while one was open for 0% of the time, Pallas kernels for 0%

profile of v1, /device:TPU:33, one launch (start us, length us, event | category | flops | bytes accessed | tf_op | source)
XLA Modules:
  0.0 296.9 jit_solution(2612423011888446278)
XLA Ops:
  0.0 0.0 copy-start
  0.0 1.6 copy.15
  1.6 1.3 constant_dynamic-slice_fusion
  3.0 0.7 pad_maximum_fusion.mine_ref
  3.6 42.4 %gather_attend.1 = bf16[128,256]{1,0:T(8,128)(2,1)} custom-call(bf16[2,128,128]{2,1,0:T(8,128)(2,1)} %bitcast.38, bf16[2,256,128]{2,1,0:T(8,128)(2,1)} %pad_maximum_fusion.mine_ref), custom_call_target="tpu_custom_call" | custom-call | tf_op jit(solution)/shard_map/gather_attend/pallas_call | solution.py:159
  46.0 0.0 copy-done
  46.0 1.3 convolution_convert_fusion.1
  47.3 0.0 copy-start.2
  47.3 1.2 reshape.63
  48.5 0.0 copy-start.3
  48.5 0.0 copy-start.1
  48.5 6.7 %all-to-all-start = ((bf16[32,4,4096]{2,1,0:T(4,128)(2,1)}), bf16[32,4,4096]{2,1,0:T(4,128)(2,1)S(1)}, u32[]{:S(2)}, u32[]{:S(2)}) async-start(bf16[32,4,4096]{2,1,0:T(4,128)(2,1)} %reshape.63), calls=%async_computation | async-start | bytes 2097152 | tf_op jit(solution)/shard_map/all_to_all | solution.py:180
  55.2 0.0 copy-done.2
  55.2 0.1 eq.13
  55.3 0.2 convert_reduce_fusion.2
  55.5 0.1 reduce_sum.70
  55.6 0.0 copy-done.3
  55.6 0.1 reduce_sum.71
  55.7 0.1 broadcast_divide_fusion
  55.8 0.1 convert_reduce_fusion.1
  55.9 16.4 %all-to-all-done = bf16[32,4,4096]{2,1,0:T(4,128)(2,1)S(1)} async-done(((bf16[32,4,4096]{2,1,0:T(4,128)(2,1)}), bf16[32,4,4096]{2,1,0:T(4,128)(2,1)S(1)}, u32[]{:S(2)}, u32[]{:S(2)}) %all-to-all-start) | async-done | bytes 1048608 | tf_op jit(solution)/shard_map/all_to_all | solution.py:180
  72.3 0.4 reduce_sum.68
  72.7 0.1 fusion.18
  72.9 0.0 copy-done.1
  72.9 0.3 convolution_convert_fusion.2
  73.2 0.2 broadcast_in_dim.9
  73.3 1.0 broadcast_in_dim.10
  74.4 130.8 %all_to_all.15 = bf16[64,2,4096]{2,1,0:T(2,128)(2,1)} all-to-all(bf16[64,2,4096]{2,1,0:T(2,128)(2,1)S(1)} %bitcast.34), channel_id=1, replica_groups=mesh['ctx'=16,'exp'=32,'tp'=2] {'exp','tp'}, dimensions={0} | all-to-all | bytes 2097152 | tf_op jit(solution)/shard_map/all_to_all | solution.py:242
  205.2 1.5 reshape.65
  206.6 2.0 fusion.4
  208.6 4.4 %convolution_convert_fusion = bf16[128,4096]{1,0:T(8,128)(2,1)} fusion(bf16[1,192,4096]{2,1,0:T(8,128)(2,1)} %param.19, bf16[128,4096]{1,0:T(8,128)(2,1)S(1)} %reshape.65, bf16[1,4096,192]{1,2,0:T(8,128)(2,1)} %param.18, f32[128,192]{0,1:T(8,128)S(1)} %fusion.4), kind=kOutput, calls=%fused_computation | convolution fusion | flops 403300352 | bytes 5341184 | tf_op jit(solution)/shard_map/dot_general | solution.py:247
  213.0 1.7 reshape.66
  214.8 80.1 %all_to_all.16 = bf16[64,2,4096]{2,1,0:T(2,128)(2,1)S(1)} all-to-all(bf16[64,2,4096]{2,1,0:T(2,128)(2,1)S(1)} %reshape.66), channel_id=1, replica_groups=mesh['ctx'=16,'exp'=32,'tp'=2] {'exp','tp'}, dimensions={0} | all-to-all | bytes 2097152 | tf_op jit(solution)/shard_map/all_to_all | solution.py:248
  294.9 1.2 convert_reduce_fusion
  296.0 0.1 reshape.69
  296.2 0.8 fusion
  (4 shorter events, 0.0 us)
Async XLA Ops:
  0.0 46.0 %copy-start = (bf16[256,4096]{1,0:T(8,128)(2,1)S(1)}, bf16[256,4096]{1,0:T(8,128)(2,1)}, u32[]{:S(2)}) copy-start(bf16[256,4096]{1,0:T(8,128)(2,1)} %param.13) | copy-start | bytes 6291460
  47.3 7.9 %copy-start.2 = (s32[4,8]{1,0:T(4,128)S(1)}, s32[4,8]{1,0:T(4,128)}, u32[]{:S(2)}) copy-start(s32[4,8]{1,0:T(4,128)} %param.15) | copy-start | bytes 388
  48.5 7.0 %copy-start.3 = (f32[4,8]{1,0:T(4,128)S(1)}, f32[4,8]{1,0:T(4,128)}, u32[]{:S(2)}) copy-start(f32[4,8]{1,0:T(4,128)} %param.16) | copy-start | bytes 388
  48.5 24.3 %copy-start.1 = (f32[4096]{0:T(1024)S(1)}, f32[4096]{0:T(1024)}, u32[]{:S(2)}) copy-start(f32[4096]{0:T(1024)} %param.14) | copy-start | bytes 49156
  48.5 23.7 %all-to-all-start = ((bf16[32,4,4096]{2,1,0:T(4,128)(2,1)}), bf16[32,4,4096]{2,1,0:T(4,128)(2,1)S(1)}, u32[]{:S(2)}, u32[]{:S(2)}) async-start(bf16[32,4,4096]{2,1,0:T(4,128)(2,1)} %reshape.63), calls=%async_computation | async-start | bytes 2097152 | tf_op jit(solution)/shard_map/all_to_all | solution.py:180

commit v2 on v1

--- a/solution.py
+++ b/solution.py
@@ -167,94 +167,277 @@
     )(q, mine)
 
 
-CAP = 2
-
-
-def split_up(shard, dim, length):
-    before, after = (shard.shape[:dim], shard.shape[dim + 1 :])
-    return jnp.moveaxis(shard.reshape(*before, length, -1, *after), dim, 0)
-
-
-def sum_at_owner(shard, axis, dim):
-    length = lax.axis_size(axis)
-    pieces = lax.all_to_all(split_up(shard, dim, length), axis, 0, 0, tiled=True)
-    return jnp.sum(pieces.astype(jnp.float32), axis=0)
-
-
-def silu_mul(gate, up):
-    return gate / (1.0 + jnp.exp(-gate)) * up
+WIDE = 4096
+HC = 2048
+MSG = HC + 128
+FF = 192
+COLS = 512
+PARTS = HC // COLS
+
+
+def experts_kernel(
+    mixed_ref, gain_ref, meta_ref, wo_hbm, wg_hbm, wu_hbm, wd_hbm, out_ref,
+    wo, wg, wu, wd, xb, acc, keep, s0, r0, s1, r1, s2, r2, xs, xr, fs, fr, hid,
+    w_sem, b_s, b_r, a_s, a_r, c_s, c_r, m_s, m_r, n_s, n_r, l_s, l_r, z_s, z_r, f_s, f_r,
+):
+    z, y, x, k = where_am_i()
+    a = x * (1 - k) + y * k
+    o = y * (1 - k) + x * k
+    other = device(z, y, x, 1 - k)
+    to_a = [None] + [device(z, y + r * k, x + r * (1 - k), k) for r in (1, 2, 3)]
+    to_b = [None] + [device(z, y + r * (1 - k), x + r * k, k) for r in (1, 2, 3)]
+    far = device(z + jnp.where(lax.rem(z // 8, 2) == 1, 8, -8), y, x, k)
+
+    def block(aa, oo):
+        aa, oo = lax.rem(aa + 4, 4), lax.rem(oo + 4, 4)
+        return oo * (4 - 3 * k) + aa * (1 + 3 * k)
+
+    me = block(a, o)
+    loads = [
+        pltpu.make_async_copy(src, dst, w_sem.at[i])
+        for i, (src, dst) in enumerate(
+            ((wo_hbm, wo), (wg_hbm.at[0], wg), (wu_hbm.at[0], wu), (wd_hbm.at[0], wd))
+        )
+    ]
+    for cp in loads:
+        cp.start()
+    sent = []
+
+    def go(cp):
+        cp.start()
+        sent.append(cp)
+
+    peers = [other, far] + to_a[1:] + to_b[1:]
+    barrier = pltpu.get_barrier_semaphore()
+    for d in peers:
+        pl.semaphore_signal(barrier, inc=1, device_id=d, device_id_type=MESH)
+
+    def rs_pair(i, j):
+        cols = pl.ds(j * COLS, COLS)
+        return remote(s0.at[i, :, :, cols], r0.at[i, :, :, cols], l_s.at[i, j], l_r.at[i, j], other)
+
+    def rs_a(i, r):
+        return remote(s1.at[i, r - 1], r1.at[i, r - 1], m_s.at[i, r - 1], m_r.at[i, r - 1], to_a[r])
+
+    def rs_b(i, r):
+        return remote(s2.at[i, r - 1], r2.at[i, r - 1], n_s.at[i, r - 1], n_r.at[i, r - 1], to_b[r])
+
+    def times(lhs, w, half, j):
+        cols = pl.ds(pl.multiple_of(half * HC + j * COLS, COLS), COLS)
+        return jnp.dot(lhs, w[:, cols], preferred_element_type=F32).reshape(16, 8, COLS)
+
+    def rs_pair_fill(i, lhs, w):
+        for j in range(PARTS):
+            s0[i, :, :, j * COLS:(j + 1) * COLS] = times(lhs, w, 1 - k, j).astype(BF16)
+
+    def rs_pair_go(i):
+        for j in range(PARTS):
+            go(rs_pair(i, j))
+
+    def rs_own(lhs, w):
+        for j in range(PARTS):
+            acc[:, :, j * COLS:(j + 1) * COLS] = times(lhs, w, k, j)
+
+    def rs_first(i):
+        for j in range(PARTS):
+            rs_pair(i, j).wait_recv()
+        for r in (2, 1, 3, 0):
+            for oo in range(4):
+                b = block(a + r, oo)
+                v = acc[b] + r0[i, b].astype(F32)
+                if r:
+                    s1[i, r - 1, oo] = v.astype(BF16)
+                else:
+                    keep[oo] = v
+            if r:
+                go(rs_a(i, r))
+
+    def rs_second(i):
+        for r in (1, 3, 2):
+            rs_a(i, r).wait_recv()
+        for r in (2, 1, 3, 0):
+            oo = lax.rem(o + r, 4)
+            v = keep[oo]
+            for q in range(3):
+                v = v + r1[i, q, oo].astype(F32)
+            if r:
+                s2[i, r - 1] = v.astype(BF16)
+                go(rs_b(i, r))
+        return v
+
+    def rs_last(i, v):
+        for r in (1, 3, 2):
+            rs_b(i, r).wait_recv()
+        for q in range(3):
+            v = v + r2[i, q].astype(F32)
+        return v
+
+    def ag_b(p, r):
+        blk = xb.at[p, k, me]
+        return remote(blk, blk, b_s.at[p, r - 1], b_r.at[p, r - 1], to_b[r])
+
+    def ag_a(p, q, r):
+        blk = xb.at[p, k, block(a, o - q)]
+        return remote(blk, blk, a_s.at[p, q, r - 1], a_r.at[p, q, r - 1], to_a[r])
+
+    def ag_c(p, q, r):
+        blk = xb.at[p, k, block(a - r, o - q)]
+        return remote(blk, blk, c_s.at[p, q, r], c_r.at[p, q, r], other)
+
+    def ag_start(p):
+        for r in (2, 1, 3):
+            go(ag_b(p, r))
+        for r in (2, 1, 3):
+            go(ag_a(p, 0, r))
+        go(ag_c(p, 0, 0))
+
+    def ag_forward(p):
+        for q in (1, 3, 2):
+            ag_b(p, q).wait_recv()
+            for r in (2, 1, 3):
+                go(ag_a(p, q, r))
+            go(ag_c(p, q, 0))
+
+    def ag_pair(p):
+        for q in (0, 1, 3, 2):
+            for r in (1, 3, 2):
+                ag_a(p, q, r).wait_recv()
+                go(ag_c(p, q, r))
+
+    def ag_wait(p):
+        for q in range(4):
+            for r in range(4):
+                ag_c(p, q, r).wait_recv()
+
+    lane = lax.broadcasted_iota(jnp.int32, (1, 128), 1)
+    expert = lax.rem((y * 4 + x) * 2 + k, 16)
+
+    def ffn(p):
+        info = xb[p, 0, :, :, HC:MSG].astype(F32) + xb[p, 1, :, :, HC:MSG].astype(F32)
+        info = info.reshape(128, 128)
+        square = jnp.sum(jnp.where(lane < 16, info, 0.0), axis=1, keepdims=True)
+        mine = (lane == 16 + expert) | (lane == 32 + expert)
+        share = jnp.sum(jnp.where(mine, info, 0.0), axis=1, keepdims=True)
+        inverse = lax.rsqrt(square * (1.0 / WIDE) + 1e-06)
+        gate = jnp.zeros((128, FF), F32)
+        up = jnp.zeros((128, FF), F32)
+        for h in range(2):
+            for j in range(PARTS):
+                v = xb[p, h, :, :, j * COLS:(j + 1) * COLS].astype(F32).reshape(128, COLS)
+                at = h * HC + j * COLS
+                v = (v * inverse * gain_ref[:, at:at + COLS]).astype(BF16)
+                gate += jnp.dot(v, wg[at:at + COLS], preferred_element_type=F32)
+                up += jnp.dot(v, wu[at:at + COLS], preferred_element_type=F32)
+        return (gate / (1.0 + jnp.exp(-gate)) * up * share).astype(BF16)
+
+    mixed = mixed_ref[...]
+    loads[0].wait()
+    rs_pair_fill(0, mixed, wo)
+    pl.semaphore_wait(barrier, len(peers))
+    rs_pair_go(0)
+    rs_own(mixed, wo)
+    rs_first(0)
+    state = rs_last(0, rs_second(0)).astype(BF16)
+    state_wide = state.astype(F32)
+    square = jnp.sum(state_wide * state_wide, axis=1, keepdims=True)
+    top = square.astype(BF16).astype(F32)
+    mid = (square - top).astype(BF16).astype(F32)
+    meta = meta_ref[...]
+    high = meta.astype(BF16).astype(F32)
+    info = jnp.where(lane < 32, high, meta - high)
+    info = jnp.where(lane == 0, top, info)
+    info = jnp.where(lane == 1, mid, info)
+    info = jnp.where(lane == 2, square - top - mid, info)
+    xb[0, k, me, :, 0:HC] = state
+    xb[0, k, me, :, HC:MSG] = info.astype(BF16)
+    cross = remote(xb.at[0, k, me], xb.at[1, k, me], z_s.at[0], z_r.at[0], far)
+    go(cross)
+    ag_start(0)
+    ag_forward(0)
+    ag_pair(0)
+    for cp in loads[1:]:
+        cp.wait()
+    ag_wait(0)
+    hid[...] = ffn(0)
+    cross.wait_recv()
+    ag_start(1)
+    ag_forward(1)
+    ag_pair(1)
+    ag_wait(1)
+    hidden = ffn(1)
+    rs_pair_fill(1, hidden, wd)
+    rs_pair_go(1)
+    rs_own(hidden, wd)
+    rs_first(1)
+    xs[...] = rs_last(1, rs_second(1)).astype(BF16)
+    back = remote(xs, xr, z_s.at[1], z_r.at[1], far)
+    go(back)
+    hidden = hid[...]
+    rs_pair_fill(2, hidden, wd)
+    rs_pair_go(2)
+    rs_own(hidden, wd)
+    rs_first(2)
+    moe = rs_last(2, rs_second(2))
+    back.wait_recv()
+    total = (state_wide + moe + xr[...].astype(F32)).astype(BF16).astype(F32)
+    low, upper = total[0:4], total[4:8]
+    fs[...] = jnp.where(k == 0, upper, low).astype(BF16)
+    swap = remote(fs, fr, f_s, f_r, other)
+    go(swap)
+    out_ref[:, pl.ds(pl.multiple_of(k * HC, HC), HC)] = jnp.where(k == 0, low, upper).astype(BF16)
+    swap.wait_recv()
+    out_ref[:, pl.ds(pl.multiple_of((1 - k) * HC, HC), HC)] = fr[...]
+    for cp in sent:
+        cp.wait_send()
+
+
+def experts(mixed, gain, meta, wo, wg, wu, wd):
+    dma = pltpu.SemaphoreType.DMA
+    vmem = pl.BlockSpec(memory_space=VMEM)
+    hbm = pl.BlockSpec(memory_space=pl.ANY)
+    return pl.pallas_call(
+        experts_kernel,
+        out_shape=jax.ShapeDtypeStruct((4, WIDE), BF16),
+        in_specs=[vmem] * 3 + [hbm] * 4,
+        out_specs=vmem,
+        scratch_shapes=[
+            VMEM((256, WIDE), BF16), VMEM((WIDE, FF), BF16), VMEM((WIDE, FF), BF16), VMEM((FF, WIDE), BF16),
+            VMEM((2, 2, 16, 8, MSG), BF16), VMEM((16, 8, HC), F32), VMEM((4, 8, HC), F32),
+            VMEM((3, 16, 8, HC), BF16), VMEM((3, 16, 8, HC), BF16),
+            VMEM((3, 3, 4, 8, HC), BF16), VMEM((3, 3, 4, 8, HC), BF16),
+            VMEM((3, 3, 8, HC), BF16), VMEM((3, 3, 8, HC), BF16),
+            VMEM((8, HC), BF16), VMEM((8, HC), BF16), VMEM((4, HC), BF16), VMEM((4, HC), BF16),
+            VMEM((128, FF), BF16),
+            dma((4,)),
+            dma((2, 3)), dma((2, 3)), dma((2, 4, 3)), dma((2, 4, 3)), dma((2, 4, 4)), dma((2, 4, 4)),
+            dma((3, 3)), dma((3, 3)), dma((3, 3)), dma((3, 3)), dma((3, PARTS)), dma((3, PARTS)),
+            dma((2,)), dma((2,)), dma, dma,
+        ],
+        compiler_params=pltpu.CompilerParams(collective_id=1, has_side_effects=True),
+        name="project_experts",
+    )(mixed, gain, meta, wo, wg, wu, wd)
 
 
 def on_device(
     queries, keys, values, out_weight, norm_gain, routes, route_weight, w_gate, w_up, w_down
 ):
     blocks, lanes, rows, local_heads, head_dim = queries.shape
-    width = out_weight.shape[1]
-    n_exp = lax.axis_size("exp")
-    n_tp = lax.axis_size("tp")
-    live_count = n_exp // 2
-    ctx_index = lax.axis_index("ctx")
-    exp_index = lax.axis_index("exp")
-    tp_index = lax.axis_index("tp")
-    group = local_heads * n_exp // keys.shape[1]
-    kv_head = exp_index * local_heads // group
+    e = lax.axis_index("exp")
+    y, k = e // 8, lax.rem(e, 2)
     mine = jnp.stack(
         [
-            lax.dynamic_index_in_dim(keys, kv_head, 1, keepdims=False),
-            lax.dynamic_index_in_dim(values, kv_head, 1, keepdims=False),
+            lax.dynamic_index_in_dim(keys, y, 1, keepdims=False),
+            lax.dynamic_index_in_dim(values, y, 1, keepdims=False),
         ]
     )
-    query_rows = blocks * rows
-    query_vector = queries.reshape(query_rows, local_heads, head_dim).transpose(1, 0, 2)
-    mixed_rows = attention(query_vector, mine)
-    summed = sum_at_owner(
-        jnp.dot(mixed_rows, out_weight, preferred_element_type=jnp.float32).astype(jnp.bfloat16),
-        "exp",
-        0,
-    )
-    state = summed.astype(jnp.bfloat16)
-    state_wide = state.astype(jnp.float32)
-    inverse = lax.rsqrt(jnp.mean(state_wide * state_wide, axis=1, keepdims=True) + 1e-06)
-    normed = (state_wide * inverse * norm_gain[None, :]).astype(jnp.bfloat16)
-    picks = routes.shape[1]
-    flat = routes.reshape(-1)
-    order = jnp.arange(flat.shape[0], dtype=jnp.int32)
-    same = (flat[:, None] == flat[None, :]) & (order[None, :] < order[:, None])
-    slot = jnp.sum(same.astype(jnp.int32), axis=1)
-    target = jnp.where(flat < live_count, flat * CAP + slot, -1)
-    slots = jnp.arange(live_count * CAP, dtype=jnp.int32)
-    hit = (
-        (target[None, :] == slots[:, None])
-        .astype(jnp.float32)
-        .reshape(live_count * CAP, rows, picks)
-    )
-    pick = jnp.sum(hit, axis=2).astype(jnp.bfloat16)
-    buffer = (
-        jnp.dot(pick, normed, preferred_element_type=jnp.float32)
-        .astype(jnp.bfloat16)
-        .reshape(live_count, CAP, width)
-    )
+    query_vector = queries.reshape(blocks * rows, local_heads, head_dim).transpose(1, 0, 2)
+    mixed = attention(query_vector, mine)
     share = route_weight / jnp.sum(route_weight, axis=1, keepdims=True)
-    mix = jnp.sum(hit * share[None, :, :], axis=2).T
-    outgoing = jnp.broadcast_to(buffer[None, :, None], (2, live_count, n_tp, CAP, width)).reshape(
-        n_exp * n_tp, CAP, width
-    )
-    received = lax.all_to_all(outgoing, ("exp", "tp"), split_axis=0, concat_axis=0, tiled=True)
-    flat_rows = received.reshape(-1, width)
-    gate = jnp.dot(flat_rows, w_gate[0], preferred_element_type=jnp.float32)
-    up = jnp.dot(flat_rows, w_up[0], preferred_element_type=jnp.float32)
-    hidden = silu_mul(gate, up).astype(jnp.bfloat16)
-    result = jnp.dot(hidden, w_down[0], preferred_element_type=jnp.float32).astype(jnp.bfloat16)
-    returned = lax.all_to_all(
-        result.reshape(received.shape), ("exp", "tp"), split_axis=0, concat_axis=0, tiled=True
-    )
-    expert_output_rows = jnp.sum(
-        returned.astype(jnp.float32).reshape(2, live_count, n_tp, CAP, width), axis=(0, 2)
-    )
-    moe = jnp.dot(
-        mix, expert_output_rows.reshape(live_count * CAP, width), preferred_element_type=jnp.float32
-    )
-    return (state_wide + moe).astype(jnp.bfloat16)
+    expert = jnp.arange(128, dtype=jnp.int32)
+    expert = jnp.where((expert >= 16) & (expert < 48), expert % 16, -1)
+    table = jnp.sum(jnp.where(routes[:, :, None] == expert[None, None, :], share[:, :, None], 0.0), axis=1)
+    meta = jnp.where((jnp.arange(8)[:, None] // 4) == k, jnp.concatenate([table, table]), 0.0)
+    return experts(mixed, norm_gain[None, :], meta, out_weight, w_gate, w_up, w_down)
 
 
 def solution(mesh):

time: 297 us -> 124 us (0.42)
  the two profiles are of different devices: /device:TPU:33 before, /device:TPU:1 now
where the time goes in v2:
time: 124 us
  Pallas kernels  111 us (90%)
  local copies, waits for them, and re-layouts  9.14 us (7%)
  other arithmetic  3.77 us (3%)
    pallas_call x1, Pallas kernels, experts(): pl.pallas_call(experts_kernel, out_shape=jax.ShapeDtypeStruct((4, WIDE),...  66.9 us
    pallas_call x1, Pallas kernels, attention(): pl.pallas_call(attention_kernel, out_shape=jax.ShapeDtypeStruct((128, 256...  44.2 us
    unnamed x10, local copies, waits for them, and re-layouts  7.83 us

profile of v2, /device:TPU:1, one launch (start us, length us, event | category | flops | bytes accessed | tf_op | source)
XLA Modules:
  0.0 124.0 jit_solution(4283735908865898531)
XLA Ops:
  0.0 0.0 copy-start
  0.0 0.9 reduce_sum.18
  0.9 0.8 broadcast_divide_fusion
  1.7 0.8 select_reduce_fusion
  2.5 0.7 maximum_select_fusion.meta_ref
  3.1 1.5 %copy.19 = bf16[32,1,4,2,128]{4,2,0,3,1:T(4,128)(2,1)} copy(bf16[32,1,4,2,128]{4,3,2,1,0:T(2,128)(2,1)} %param.10) | data formatting | bytes 131072 | tf_op args[0]
  4.6 1.3 %constant_dynamic-slice_fusion = (bf16[256,1,128]{2,1,0:T(2,128)(2,1)S(1)}, bf16[256,1,128]{2,1,0:T(2,128)(2,1)S(1)}) fusion(bf16[256,4,128]{2,1,0:T(4,128)(2,1)} %param.12, s32[]{:T(128)S(6)} %select_n.47, bf16[256,4,128]{2,1,0:T(4,128)(2,1)} %param.11), kind=kLoop, calls=%fused_computation.14 | loop fusion | bytes 262148 | tf_op jit(solution)/shard_map/jit(dynamic_index_in_dim)/dynamic_slice | solution.py:430
  5.9 0.0 copy-start.1
  6.0 0.7 pad_maximum_fusion.mine_ref
  6.6 44.2 %gather_attend.1.mixed_ref = bf16[128,256]{1,0:T(8,128)(2,1)} custom-call(bf16[2,128,128]{2,1,0:T(8,128)(2,1)} %bitcast.12, bf16[2,256,128]{2,1,0:T(8,128)(2,1)} %pad_maximum_fusion.mine_ref), custom_call_target="tpu_custom_call" | custom-call | tf_op jit(solution)/shard_map/gather_attend/pallas_call | solution.py:159
  50.8 0.0 copy-done
  50.8 2.5 %copy.22.wg_hbm = bf16[1,4096,192]{2,1,0:T(8,128)(2,1)} copy(bf16[1,4096,192]{1,2,0:T(8,128)(2,1)S(1)} %copy-done) | data formatting | bytes 3145728 | tf_op args[7]
  53.3 0.0 copy-done.1
  53.3 2.5 %copy.23.wu_hbm = bf16[1,4096,192]{2,1,0:T(8,128)(2,1)} copy(bf16[1,4096,192]{1,2,0:T(8,128)(2,1)S(1)} %copy-done.1) | data formatting | bytes 3145728 | tf_op args[8]
  55.8 66.9 %project_experts.1 = bf16[4,4096]{1,0:T(4,128)(2,1)} custom-call(bf16[128,256]{1,0:T(8,128)(2,1)} %gather_attend.1.mixed_ref, f32[1,4096]{1,0:T(1,128)} %bitcast.13, f32[8,128]{1,0:T(8,128)} %maximum_select_fusion.meta_ref, bf16[256,4096]{1,0:T(8,128)(2,1)} %wo_hbm.1, bf16[1,4096,192]{2,1,0:T(8,128)(2,1)} %copy.22.wg_hbm, ...), custom_call_target="tpu_custom_call" | custom-call | tf_op jit(solution)/shard_map/project_experts/pallas_call | solution.py:398
  122.6 1.4 %copy.31 = bf16[4,4096]{1,0:T(4,128)(2,1)} copy(bf16[4,4096]{1,0:T(4,128)(2,1)} %project_experts.1) | data formatting | bytes 65536
  (4 shorter events, 0.0 us)
Async XLA Ops:
  0.0 50.8 %copy-start = (bf16[1,4096,192]{1,2,0:T(8,128)(2,1)S(1)}, bf16[1,4096,192]{1,2,0:T(8,128)(2,1)}, u32[]{:S(2)}) copy-start(bf16[1,4096,192]{1,2,0:T(8,128)(2,1)} %param.17) | copy-start | bytes 4718596
  5.9 47.4 %copy-start.1 = (bf16[1,4096,192]{1,2,0:T(8,128)(2,1)S(1)}, bf16[1,4096,192]{1,2,0:T(8,128)(2,1)}, u32[]{:S(2)}) copy-start(bf16[1,4096,192]{1,2,0:T(8,128)(2,1)} %param.18) | copy-start | bytes 4718596

commit v3 on v2

v3 whole, which is shorter than its diff:
```python
import functools
import jax
import jax.numpy as jnp
from jax import lax
from jax.experimental import pallas as pl
from jax.experimental.pallas import tpu as pltpu
from jax.sharding import PartitionSpec as P

MESH = pl.DeviceIdType.MESH
VMEM = pltpu.VMEM
F32 = jnp.float32
BF16 = jnp.bfloat16
CHUNK = 256
HALF = 128
NC = 16


def where_am_i():
    c = lax.axis_index("ctx")
    e = lax.axis_index("exp")
    t = lax.axis_index("tp")
    return t * NC + c, e // 8, lax.rem(e // 2, 4), lax.rem(e, 2)


def device(z, y, x, k):
    z = lax.rem(z + 2 * NC, 2 * NC)
    y = lax.rem(y + 4, 4)
    x = lax.rem(x + 4, 4)
    return (lax.rem(z, NC), (y * 4 + x) * 2 + k, z // NC)


def remote(src, dst, ssem, rsem, dev):
    return pltpu.make_async_remote_copy(
        src_ref=src, dst_ref=dst, send_sem=ssem, recv_sem=rsem, device_id=dev, device_id_type=MESH
    )


WIDE = 4096
HC = 2048
MSG = HC + 128
FF = 192
COLS = 512
PARTS = HC // COLS
NT = (((1,), (1,)), ((), ()))


def when(cond):
    return pl.when(cond)


def layer_kernel(
    routes_ref, weight_ref, gain_ref, q_hbm, k_hbm, v_hbm, wo_hbm, wg_hbm, wu_hbm, wd_hbm, out_ref,
    qv, kin, wide, mine, kv, mx, den, mixacc, pairs,
    wo, wg, wu, wd, xb, acc, keep, s0, r0, s1, r1, s2, r2, xs, xr, fs, fr, first_moe,
    in_sem, hu, hd, up_s, up_r, dn_s, dn_r, x_s, x_r, g_s, g_r,
    b_s, b_r, a_s, a_r, c_s, c_r, m_s, m_r, n_s, n_r, l_s, l_r, z_s, z_r, f_s, f_r,
):
    z, y, x, k = where_am_i()
    c = lax.axis_index("ctx")
    t = lax.axis_index("tp")
    half = lax.rem(x, 2)
    a = x * (1 - k) + y * k
    o = y * (1 - k) + x * k
    other = device(z, y, x, 1 - k)
    beside = device(z, y, x + 1 - 2 * half, k)
    up1, up2 = device(z + 1, y, x, k), device(z + 2, y, x, k)
    dn1, dn2 = device(z - 1, y, x, k), device(z - 2, y, x, k)
    to_a = [None] + [device(z, y + r * k, x + r * (1 - k), k) for r in (1, 2, 3)]
    to_b = [None] + [device(z, y + r * (1 - k), x + r * k, k) for r in (1, 2, 3)]
    far = device(z + jnp.where(lax.rem(z // 8, 2) == 1, 8, -8), y, x, k)

    peers = [up1, up2, dn1, dn2, other] + to_a[1:] + to_b[1:]
    barrier = pltpu.get_barrier_semaphore()
    for d in peers:
        pl.semaphore_signal(barrier, inc=1, device_id=d, device_id_type=MESH)
    loads = [
        pltpu.make_async_copy(src, dst, in_sem.at[i])
        for i, (src, dst) in enumerate(
            (
                (k_hbm, kin.at[0]), (v_hbm, kin.at[1]), (q_hbm, qv), (wo_hbm, wo),
                (wg_hbm.at[0], wg), (wu_hbm.at[0], wu), (wd_hbm.at[0], wd),
            )
        )
    ]
    for cp in loads:
        cp.start()
    sent = []

    def go(cp):
        cp.start()
        sent.append(cp)

    def block(aa, oo):
        aa, oo = lax.rem(aa + 4, 4), lax.rem(oo + 4, 4)
        return oo * (4 - 3 * k) + aa * (1 + 3 * k)

    me = block(a, o)

    def piece(pos):
        return kv.at[k, pos, half]

    def slot_up(d):
        return 2 * (d - 1)

    def slot_dn(d):
        return 2 * (d - 1) + 1

    own = mine.at[k, pl.ds(half * HALF, HALF)]
    ups, dns = [None], [None]
    for d in range(1, 9):
        src = own if d < 3 else piece(slot_up(d - 2))
        ups.append(remote(src, piece(slot_up(d)), up_s.at[d - 1], up_r.at[d - 1], up1 if d == 1 else up2))
    for d in range(1, 8):
        src = own if d < 3 else piece(slot_dn(d - 2))
        dns.append(remote(src, piece(slot_dn(d)), dn_s.at[d - 1], dn_r.at[d - 1], dn1 if d == 1 else dn2))
    xc = [remote(piece(p), piece(p), x_s.at[p], x_r.at[p], beside) for p in range(15)]
    gc = [remote(kv.at[k, p], kv.at[k, p], g_s.at[p], g_r.at[p], other) for p in range(15)]

    def sends_up(d):
        return c + d <= 15 if d < 3 else (c >= d - 2) & (c <= 13)

    def has_up(d):
        return c >= d

    def has_dn(d):
        return lax.rem(c + d, NC) < (7 if d % 2 else 6)

    def sends_dn(d):
        return c < (7 if d == 1 else 6) if d < 3 else has_dn(d - 2)

    def needs_dn(d):
        return c + d >= NC

    loads[0].wait()
    loads[1].wait()
    for i in range(2):
        wide[i] = kin[i].astype(F32)
        mine[i] = wide[i, pl.ds(y, CHUNK, stride=4), :].astype(BF16)
    pl.semaphore_wait(barrier, len(peers))
    when(sends_up(1))(ups[1].start)
    when(sends_dn(1))(dns[1].start)
    when(sends_up(2))(ups[2].start)
    when(sends_dn(2))(dns[2].start)
    pl.semaphore_signal(hu.at[0], inc=1, device_id=up2, device_id_type=MESH)
    pl.semaphore_signal(hd.at[0], inc=1, device_id=dn2, device_id_type=MESH)

    scale = 128 ** (-0.5)
    loads[2].wait()

    def scores(keys):
        return lax.dot_general(qv[...], keys, NT, preferred_element_type=F32) * scale

    def mix(prob, vals):
        return jnp.dot(prob.astype(BF16), vals, preferred_element_type=F32)

    s = scores(mine[0])
    row = lax.broadcasted_iota(jnp.int32, (256, CHUNK), 0) >> 1
    col = lax.broadcasted_iota(jnp.int32, (256, CHUNK), 1)
    ok = col <= ((row >> 2) * 2 + t) * 4 + (row & 3)
    s = jnp.where(ok, s, -1e30)
    m = jnp.max(s, axis=1, keepdims=True)
    e = jnp.where(ok, jnp.exp(s - m), 0.0)
    mx[...] = m
    den[...] = jnp.sum(e, axis=1, keepdims=True)
    mixacc[...] = mix(e, mine[1])

    def z_stage(d):
        @when(has_up(d))
        def _():
            ups[d].wait_recv()
            if d + 2 <= 8:
                when(c <= 13)(ups[d + 2].start)
            xc[slot_up(d)].start()

        if d <= 7:
            @when(has_dn(d))
            def _():
                dns[d].wait_recv()
                if d + 2 <= 7:
                    dns[d + 2].start()
                when(needs_dn(d))(xc[slot_dn(d)].start)

    def x_stage(d):
        @when(has_up(d))
        def _():
            xc[slot_up(d)].wait_recv()
            gc[slot_up(d)].start()

        if d <= 7:
            @when(needs_dn(d))
            def _():
                xc[slot_dn(d)].wait_recv()
                gc[slot_dn(d)].start()

    def absorb_one(p):
        gc[p].wait_recv()
        s = scores(kv[0, p].reshape(CHUNK, 128))
        m = mx[...]
        m_new = jnp.maximum(m, jnp.max(s, axis=1, keepdims=True))
        fade = jnp.exp(m - m_new)
        e = jnp.exp(s - m_new)
        mx[...] = m_new
        den[...] = den[...] * fade + jnp.sum(e, axis=1, keepdims=True)
        mixacc[...] = mixacc[...] * fade + mix(e, kv[1, p].reshape(CHUNK, 128))

    def absorb(d):
        when(has_up(d))(functools.partial(absorb_one, slot_up(d)))
        if d <= 7:
            when(needs_dn(d))(functools.partial(absorb_one, slot_dn(d)))

    def hello(j):
        pl.semaphore_wait(hu.at[j], 1)
        if j < 2:
            pl.semaphore_signal(hu.at[j + 1], inc=1, device_id=up2, device_id_type=MESH)
        pl.semaphore_wait(hd.at[j], 1)
        if j < 2:
            pl.semaphore_signal(hd.at[j + 1], inc=1, device_id=dn2, device_id_type=MESH)

    for i in range(1, 11):
        if i <= 8:
            z_stage(i)
        if 1 <= i - 1 <= 8:
            x_stage(i - 1)
        if i in (3, 5, 8):
            hello({3: 0, 5: 1, 8: 2}[i])
        if 1 <= i - 2 <= 8:
            absorb(i - 2)
    pairs[...] = mixacc[...] / den[...]

    def rs_pair(i, j):
        cols = pl.ds(j * COLS, COLS)
        return remote(s0.at[i, :, :, cols], r0.at[i, :, :, cols], l_s.at[i, j], l_r.at[i, j], other)

    def rs_a(i, r):
        return remote(s1.at[i, r - 1], r1.at[i, r - 1], m_s.at[i, r - 1], m_r.at[i, r - 1], to_a[r])

    def rs_b(i, r):
        return remote(s2.at[i, r - 1], r2.at[i, r - 1], n_s.at[i, r - 1], n_r.at[i, r - 1], to_b[r])

    def times(lhs, w, half, j):
        cols = pl.ds(pl.multiple_of(half * HC + j * COLS, COLS), COLS)
        return jnp.dot(lhs, w[:, cols], preferred_element_type=F32).reshape(16, 8, COLS)

    def rs_pair_fill(i, lhs, w):
        for j in range(PARTS):
            s0[i, :, :, j * COLS:(j + 1) * COLS] = times(lhs, w, 1 - k, j).astype(BF16)

    def rs_pair_go(i):
        for j in range(PARTS):
            go(rs_pair(i, j))

    def rs_own(lhs, w):
        for j in range(PARTS):
            acc[:, :, j * COLS:(j + 1) * COLS] = times(lhs, w, k, j)

    def rs_first(i):
        for j in range(PARTS):
            rs_pair(i, j).wait_recv()
        for r in (2, 1, 3, 0):
            for oo in range(4):
                b = block(a + r, oo)
                v = acc[b] + r0[i, b].astype(F32)
                if r:
                    s1[i, r - 1, oo] = v.astype(BF16)
                else:
                    keep[oo] = v
            if r:
                go(rs_a(i, r))

    def rs_second(i):
        for r in (1, 3, 2):
            rs_a(i, r).wait_recv()
        for r in (2, 1, 3, 0):
            oo = lax.rem(o + r, 4)
            v = keep[oo]
            for q in range(3):
                v = v + r1[i, q, oo].astype(F32)
            if r:
                s2[i, r - 1] = v.astype(BF16)
                go(rs_b(i, r))
        return v

    def rs_last(i, v):
        for r in (1, 3, 2):
            rs_b(i, r).wait_recv()
        for q in range(3):
            v = v + r2[i, q].astype(F32)
        return v

    def ag_b(p, r):
        blk = xb.at[p, k, me]
        return remote(blk, blk, b_s.at[p, r - 1], b_r.at[p, r - 1], to_b[r])

    def ag_a(p, q, r):
        blk = xb.at[p, k, block(a, o - q)]
        return remote(blk, blk, a_s.at[p, q, r - 1], a_r.at[p, q, r - 1], to_a[r])

    def ag_c(p, q, r):
        blk = xb.at[p, k, block(a - r, o - q)]
        return remote(blk, blk, c_s.at[p, q, r], c_r.at[p, q, r], other)

    def ag_start(p):
        for r in (2, 1, 3):
            ag_b(p, r).start()
        for r in (2, 1, 3):
            ag_a(p, 0, r).start()
        ag_c(p, 0, 0).start()

    def ag_forward(p):
        for q in (1, 3, 2):
            ag_b(p, q).wait_recv()
            for r in (2, 1, 3):
                ag_a(p, q, r).start()
            ag_c(p, q, 0).start()

    def ag_pair(p):
        for q in (0, 1, 3, 2):
            for r in (1, 3, 2):
                ag_a(p, q, r).wait_recv()
                ag_c(p, q, r).start()

    def ag_wait(p):
        for q in range(4):
            for r in range(4):
                ag_c(p, q, r).wait_recv()

    lane = lax.broadcasted_iota(jnp.int32, (1, 128), 1)
    expert = lax.rem((y * 4 + x) * 2 + k, 16)

    def ffn_half(p, h, gate, up):
        for j in range(PARTS):
            at = pl.ds(pl.multiple_of(h * HC + j * COLS, COLS), COLS)
            v = xb[p, h, :, :, j * COLS:(j + 1) * COLS].astype(F32).reshape(128, COLS)
            v = (v * gain_ref[:, at]).astype(BF16)
            gate = gate + lax.dot_general(v, wg[:, at], NT, preferred_element_type=F32)
            up = up + lax.dot_general(v, wu[:, at], NT, preferred_element_type=F32)
        return gate, up

    def ffn(p):
        zero = jnp.zeros((128, FF), F32)
        gate, up = ffn_half(p, k, zero, zero)
        ag_wait(p)
        gate, up = ffn_half(p, 1 - k, gate, up)
        info = xb[p, 0, :, :, HC:MSG].astype(F32) + xb[p, 1, :, :, HC:MSG].astype(F32)
        info = info.reshape(128, 128)
        square = jnp.sum(jnp.where(lane < 16, info, 0.0), axis=1, keepdims=True)
        chosen = (lane == 16 + expert) | (lane == 32 + expert)
        share = jnp.sum(jnp.where(chosen, info, 0.0), axis=1, keepdims=True)
        inverse = lax.rsqrt(square * (1.0 / WIDE) + 1e-06)
        gate, up = gate * inverse, up * inverse
        return (gate / (1.0 + jnp.exp(-gate)) * up * share).astype(BF16)

    mixed = jnp.concatenate(
        [pairs[pl.ds(0, 128, stride=2), :], pairs[pl.ds(1, 128, stride=2), :]], axis=1
    ).astype(BF16)
    loads[3].wait()
    rs_pair_fill(0, mixed, wo)
    rs_pair_go(0)
    rs_own(mixed, wo)
    rs_first(0)
    share = weight_ref[...]
    share = share / jnp.sum(share, axis=1, keepdims=True)
    label = jnp.where((lane >= 16) & (lane < 48), lane & 15, -1)
    table = jnp.zeros((4, 128), F32)
    for j in range(8):
        table = table + jnp.where(routes_ref[:, j:j + 1] == label, share[:, j:j + 1], 0.0)
    rows8 = lax.broadcasted_iota(jnp.int32, (8, 128), 0)
    meta = jnp.where((rows8 >> 2) == k, jnp.concatenate([table, table], axis=0), 0.0)
    high = meta.astype(BF16).astype(F32)
    meta = jnp.where(lane < 32, high, meta - high)
    state = rs_last(0, rs_second(0)).astype(BF16)
    state_wide = state.astype(F32)
    square = jnp.sum(state_wide * state_wide, axis=1, keepdims=True)
    top = square.astype(BF16).astype(F32)
    mid = (square - top).astype(BF16).astype(F32)
    info = jnp.where(lane == 0, top, meta)
    info = jnp.where(lane == 1, mid, info)
    info = jnp.where(lane == 2, square - top - mid, info)
    xb[0, k, me, :, 0:HC] = state
    xb[0, k, me, :, HC:MSG] = info.astype(BF16)
    cross = remote(xb.at[0, k, me], xb.at[1, k, me], z_s.at[0], z_r.at[0], far)
    go(cross)
    ag_start(0)
    for cp in loads[4:]:
        cp.wait()
    begin = t

    def enter():
        cross.wait_recv()
        ag_start(1)

    def second():
        ag_forward(0)
        ag_pair(0)

    when(t == 1)(enter)
    ag_forward(begin)
    ag_pair(begin)
    when(t == 1)(second)
    hidden = ffn(begin)
    rs_pair_fill(1, hidden, wd)
    rs_pair_go(1)
    rs_own(hidden, wd)
    when(t == 0)(enter)
    rs_first(1)
    when(t == 0)(functools.partial(ag_forward, 1))
    v = rs_second(1)
    when(t == 0)(functools.partial(ag_pair, 1))
    v = rs_last(1, v)
    first_moe[...] = v
    back = remote(xs, xr, z_s.at[1], z_r.at[1], far)

    @when(t == 1)
    def _():
        xs[...] = v.astype(BF16)
        back.start()

    hidden = ffn(1 - begin)
    rs_pair_fill(2, hidden, wd)
    rs_pair_go(2)
    rs_own(hidden, wd)
    rs_first(2)
    last = rs_last(2, rs_second(2))

    @when(t == 0)
    def _():
        xs[...] = last.astype(BF16)
        back.start()

    moe = jnp.where(t == 0, first_moe[...], last)
    back.wait_recv()
    total = (state_wide + moe + xr[...].astype(F32)).astype(BF16).astype(F32)
    low, upper = total[0:4], total[4:8]
    fs[...] = jnp.where(k == 0, upper, low).astype(BF16)
    swap = remote(fs, fr, f_s, f_r, other)
    swap.start()
    out_ref[:, pl.ds(pl.multiple_of(k * HC, HC), HC)] = jnp.where(k == 0, low, upper).astype(BF16)
    swap.wait_recv()
    out_ref[:, pl.ds(pl.multiple_of((1 - k) * HC, HC), HC)] = fr[...]
    for d in range(1, 9):
        when(sends_up(d))(ups[d].wait_send)
        when(has_up(d))(xc[slot_up(d)].wait_send)
        when(has_up(d))(gc[slot_up(d)].wait_send)
        if d <= 7:
            when(sends_dn(d))(dns[d].wait_send)
            when(needs_dn(d))(xc[slot_dn(d)].wait_send)
            when(needs_dn(d))(gc[slot_dn(d)].wait_send)
    swap.wait_send()
    back.wait_send()
    for p in range(2):
        for q in range(4):
            ag_c(p, q, 0).wait_send()
            for r in (1, 2, 3):
                ag_a(p, q, r).wait_send()
                ag_c(p, q, r).wait_send()
        for r in (1, 2, 3):
            ag_b(p, r).wait_send()
    for cp in sent:
        cp.wait_send()


def layer(routes, weight, gain, q, keys, values, wo, wg, wu, wd):
    dma = pltpu.SemaphoreType.DMA
    vmem = pl.BlockSpec(memory_space=VMEM)
    hbm = pl.BlockSpec(memory_space=pl.ANY)
    return pl.pallas_call(
        layer_kernel,
        out_shape=jax.ShapeDtypeStruct((4, WIDE), BF16),
        in_specs=[vmem] * 3 + [hbm] * 7,
        out_specs=vmem,
        scratch_shapes=[
            VMEM((256, 128), BF16), VMEM((2, 1024, 128), BF16), VMEM((2, 1024, 128), F32),
            VMEM((2, CHUNK, 128), BF16), VMEM((2, 15, 2, HALF, 128), BF16),
            VMEM((256, 1), F32), VMEM((256, 1), F32), VMEM((256, 128), F32), VMEM((256, 128), F32),
            VMEM((256, WIDE), BF16), VMEM((FF, WIDE), BF16), VMEM((FF, WIDE), BF16), VMEM((FF, WIDE), BF16),
            VMEM((2, 2, 16, 8, MSG), BF16), VMEM((16, 8, HC), F32), VMEM((4, 8, HC), F32),
            VMEM((3, 16, 8, HC), BF16), VMEM((3, 16, 8, HC), BF16),
            VMEM((3, 3, 4, 8, HC), BF16), VMEM((3, 3, 4, 8, HC), BF16),
            VMEM((3, 3, 8, HC), BF16), VMEM((3, 3, 8, HC), BF16),
            VMEM((8, HC), BF16), VMEM((8, HC), BF16), VMEM((4, HC), BF16), VMEM((4, HC), BF16),
            VMEM((8, HC), F32),
            dma((7,)), pltpu.SemaphoreType.REGULAR((3,)), pltpu.SemaphoreType.REGULAR((3,)),
            dma((8,)), dma((8,)), dma((7,)), dma((7,)), dma((15,)), dma((15,)), dma((15,)), dma((15,)),
            dma((2, 3)), dma((2, 3)), dma((2, 4, 3)), dma((2, 4, 3)), dma((2, 4, 4)), dma((2, 4, 4)),
            dma((3, 3)), dma((3, 3)), dma((3, 3)), dma((3, 3)), dma((3, PARTS)), dma((3, PARTS)),
            dma((2,)), dma((2,)), dma, dma,
        ],
        compiler_params=pltpu.CompilerParams(collective_id=0, has_side_effects=True),
        name="layer",
    )(routes, weight, gain, q, keys, values, wo, wg, wu, wd)


def on_device(
    queries, keys, values, out_weight, norm_gain, routes, route_weight, w_gate, w_up, w_down
):
    return layer(
        routes, route_weight, norm_gain[None, :],
        queries.reshape(256, 128), keys.reshape(1024, 128), values.reshape(1024, 128),
        out_weight, w_gate.swapaxes(1, 2), w_up.swapaxes(1, 2), w_down,
    )


def solution(mesh):
    in_specs = (
        P("ctx", "tp", None, "exp", None),
        P("ctx", None, None),
        P("ctx", None, None),
        P("exp", None),
        P(),
        P(("ctx", "exp", "tp"), None),
        P(("ctx", "exp", "tp"), None),
        P("exp", None, "tp"),
        P("exp", None, "tp"),
        P("exp", "tp", None),
    )
    out_specs = P(("ctx", "exp", "tp"), None)
    return jax.shard_map(
        on_device, mesh=mesh, in_specs=in_specs, out_specs=out_specs, check_vma=False
    )
```

time: 124 us -> 96.9 us (0.78)
  Pallas kernels: 111 us -> 95 us
  local copies, waits for them, and re-layouts: 9.14 us -> 1.39 us
  other arithmetic: 3.77 us -> 0 us
    pallas_call x2 -> x1, Pallas kernels: 111 us -> 95 us  [layer(): pl.pallas_call(layer_kernel, out_shape=jax.ShapeDtypeStruct((4, WIDE), BF...]
    unnamed x10 -> x1, local copies, waits for them, and re-layouts: 7.83 us -> 1.39 us
    reduce_sum x2 -> x0, other arithmetic: 1.69 us -> none  [the longest x1 0.92 us: on_device(): share = route_weight / jnp.sum(route_weight, axis=1, keepdims=True)]
    dynamic_slice x1 -> x0, local copies, waits for them, and re-layouts: 1.3 us -> none  [on_device(): lax.dynamic_index_in_dim(values, y, 1, keepdims=False)]
where the time goes in v3:
time: 96.9 us; the launch traced here: 96.4 us
  Pallas kernels  95 us (98%)
  local copies, waits for them, and re-layouts  1.39 us (1%)
    pallas_call x1, Pallas kernels, layer(): pl.pallas_call(layer_kernel, out_shape=jax.ShapeDtypeStruct((4, WIDE), BF...  95 us

profile of v3, /device:TPU:1, one launch (start us, length us, event | category | flops | bytes accessed | tf_op | source)
XLA Modules:
  0.0 96.4 jit_solution(10693681581513008087)
XLA Ops:
  0.0 95.0 %layer.1 = bf16[4,4096]{1,0:T(4,128)(2,1)} custom-call(s32[4,8]{1,0:T(4,128)} %routes_ref.1, f32[4,8]{1,0:T(4,128)} %weight_ref.1, f32[1,4096]{1,0:T(1,128)} %bitcast.11, bf16[256,128]{1,0:T(8,128)(2,1)} %bitcast.10, bf16[1024,128]{1,0:T(8,128)(2,1)} %bitcast.8, bf16[1024,128]{1,0:T(8,128)(2,1)} %bitcast.9, bf16[256,4096]{1,0:T(8,128)(2,1)} %wo_hbm.1, ...), custom_call_target="tpu_custom_call" | custom-call | tf_op jit(solution)/shard_map/layer/pallas_call | solution.py:466
  95.0 1.4 %copy.12 = bf16[4,4096]{1,0:T(4,128)(2,1)} copy(bf16[4,4096]{1,0:T(4,128)(2,1)} %layer.1) | data formatting | bytes 65536

commit v4 on v3

--- a/solution.py
+++ b/solution.py
@@ -41,6 +41,9 @@
 FF = 192
 COLS = 512
 PARTS = HC // COLS
+GC = 1024
+SPLIT = GC // COLS
+GROUPS = HC // GC
 NT = (((1,), (1,)), ((), ()))
 
 
@@ -192,21 +195,35 @@
                 xc[slot_dn(d)].wait_recv()
                 gc[slot_dn(d)].start()
 
-    def absorb_one(p):
-        gc[p].wait_recv()
-        s = scores(kv[0, p].reshape(CHUNK, 128))
-        m = mx[...]
-        m_new = jnp.maximum(m, jnp.max(s, axis=1, keepdims=True))
-        fade = jnp.exp(m - m_new)
-        e = jnp.exp(s - m_new)
-        mx[...] = m_new
-        den[...] = den[...] * fade + jnp.sum(e, axis=1, keepdims=True)
-        mixacc[...] = mixacc[...] * fade + mix(e, kv[1, p].reshape(CHUNK, 128))
-
-    def absorb(d):
-        when(has_up(d))(functools.partial(absorb_one, slot_up(d)))
-        if d <= 7:
-            when(needs_dn(d))(functools.partial(absorb_one, slot_dn(d)))
+    def absorb(ds):
+        slots = []
+        for d in ds:
+            slots.append((slot_up(d), has_up(d)))
+            if d <= 7:
+                slots.append((slot_dn(d), needs_dn(d)))
+
+        @when(has_up(ds[0]))
+        def _():
+            for p, needed in slots:
+                when(needed)(gc[p].wait_recv)
+            n = len(slots)
+            keys = kv[0, pl.ds(slots[0][0], n)].reshape(n * CHUNK, 128)
+            lane = lax.broadcasted_iota(jnp.int32, (1, n * CHUNK), 1)
+            valid = jnp.zeros((1, n * CHUNK), jnp.int32)
+            vals = []
+            for j, (p, needed) in enumerate(slots):
+                flag = jnp.where(needed, 1, 0)
+                valid = jnp.where((lane >> 8) == j, flag, valid)
+                v = kv[1, p].reshape(CHUNK, 128)
+                vals.append(jnp.where(flag == 1, v, jnp.zeros_like(v)))
+            s = jnp.where(valid == 1, scores(keys), -1e30)
+            m = mx[...]
+            m_new = jnp.maximum(m, jnp.max(s, axis=1, keepdims=True))
+            fade = jnp.exp(m - m_new)
+            e = jnp.exp(s - m_new)
+            mx[...] = m_new
+            den[...] = den[...] * fade + jnp.sum(e, axis=1, keepdims=True)
+            mixacc[...] = mixacc[...] * fade + mix(e, jnp.concatenate(vals, axis=0))
 
     def hello(j):
         pl.semaphore_wait(hu.at[j], 1)
@@ -216,75 +233,76 @@
         if j < 2:
             pl.semaphore_signal(hd.at[j + 1], inc=1, device_id=dn2, device_id_type=MESH)
 
-    for i in range(1, 11):
+    for i in range(1, 10):
         if i <= 8:
             z_stage(i)
-        if 1 <= i - 1 <= 8:
+        if i >= 2:
             x_stage(i - 1)
-        if i in (3, 5, 8):
-            hello({3: 0, 5: 1, 8: 2}[i])
-        if 1 <= i - 2 <= 8:
-            absorb(i - 2)
+        if i in (1, 2):
+            hello(i - 1)
+        if i in (4, 6, 8):
+            absorb((i - 3, i - 2))
+    absorb((7,))
+    absorb((8,))
     pairs[...] = mixacc[...] / den[...]
 
     def rs_pair(i, j):
         cols = pl.ds(j * COLS, COLS)
         return remote(s0.at[i, :, :, cols], r0.at[i, :, :, cols], l_s.at[i, j], l_r.at[i, j], other)
 
-    def rs_a(i, r):
-        return remote(s1.at[i, r - 1], r1.at[i, r - 1], m_s.at[i, r - 1], m_r.at[i, r - 1], to_a[r])
-
-    def rs_b(i, r):
-        return remote(s2.at[i, r - 1], r2.at[i, r - 1], n_s.at[i, r - 1], n_r.at[i, r - 1], to_b[r])
+    def rs_a(i, g, r):
+        n = (i, g, r - 1)
+        return remote(s1.at[n], r1.at[n], m_s.at[n], m_r.at[n], to_a[r])
+
+    def rs_b(i, g, r):
+        n = (i, g, r - 1)
+        return remote(s2.at[n], r2.at[n], n_s.at[n], n_r.at[n], to_b[r])
 
     def times(lhs, w, half, j):
         cols = pl.ds(pl.multiple_of(half * HC + j * COLS, COLS), COLS)
         return jnp.dot(lhs, w[:, cols], preferred_element_type=F32).reshape(16, 8, COLS)
 
-    def rs_pair_fill(i, lhs, w):
+    def rs_pair_send(i, lhs, w):
         for j in range(PARTS):
             s0[i, :, :, j * COLS:(j + 1) * COLS] = times(lhs, w, 1 - k, j).astype(BF16)
-
-    def rs_pair_go(i):
-        for j in range(PARTS):
             go(rs_pair(i, j))
 
-    def rs_own(lhs, w):
-        for j in range(PARTS):
+    def rs_first(i, g, lhs, w):
+        for j in range(g * SPLIT, (g + 1) * SPLIT):
             acc[:, :, j * COLS:(j + 1) * COLS] = times(lhs, w, k, j)
-
-    def rs_first(i):
-        for j in range(PARTS):
+        for j in range(g * SPLIT, (g + 1) * SPLIT):
             rs_pair(i, j).wait_recv()
+        cols = slice(g * GC, (g + 1) * GC)
         for r in (2, 1, 3, 0):
             for oo in range(4):
                 b = block(a + r, oo)
-                v = acc[b] + r0[i, b].astype(F32)
+                v = acc[b, :, cols] + r0[i, b, :, cols].astype(F32)
                 if r:
-                    s1[i, r - 1, oo] = v.astype(BF16)
+                    s1[i, g, r - 1, oo] = v.astype(BF16)
                 else:
-                    keep[oo] = v
+                    keep[oo, :, cols] = v
             if r:
-                go(rs_a(i, r))
-
-    def rs_second(i):
+                go(rs_a(i, g, r))
+
+    def rs_second(i, g):
         for r in (1, 3, 2):
-            rs_a(i, r).wait_recv()
+            rs_a(i, g, r).wait_recv()
+        cols = slice(g * GC, (g + 1) * GC)
         for r in (2, 1, 3, 0):
             oo = lax.rem(o + r, 4)
-            v = keep[oo]
+            v = keep[oo, :, cols]
             for q in range(3):
-                v = v + r1[i, q, oo].astype(F32)
+                v = v + r1[i, g, q, oo].astype(F32)
             if r:
-                s2[i, r - 1] = v.astype(BF16)
-                go(rs_b(i, r))
+                s2[i, g, r - 1] = v.astype(BF16)
+                go(rs_b(i, g, r))
         return v
 
-    def rs_last(i, v):
+    def rs_last(i, g, v):
         for r in (1, 3, 2):
-            rs_b(i, r).wait_recv()
+            rs_b(i, g, r).wait_recv()
         for q in range(3):
-            v = v + r2[i, q].astype(F32)
+            v = v + r2[i, g, q].astype(F32)
         return v
 
     def ag_b(p, r):
@@ -350,14 +368,22 @@
         gate, up = gate * inverse, up * inverse
         return (gate / (1.0 + jnp.exp(-gate)) * up * share).astype(BF16)
 
+    late = c >= 8
+    early = c < 8
+    begin = jnp.where(late, 1, 0)
+    cross = remote(xb.at[0, k, me], xb.at[1, k, me], z_s.at[0], z_r.at[0], far)
+
+    def enter():
+        cross.wait_recv()
+        ag_start(1)
+
     mixed = jnp.concatenate(
         [pairs[pl.ds(0, 128, stride=2), :], pairs[pl.ds(1, 128, stride=2), :]], axis=1
     ).astype(BF16)
     loads[3].wait()
-    rs_pair_fill(0, mixed, wo)
-    rs_pair_go(0)
-    rs_own(mixed, wo)
-    rs_first(0)
+    rs_pair_send(0, mixed, wo)
+    for g in range(GROUPS):
+        rs_first(0, g, mixed, wo)
     share = weight_ref[...]
     share = share / jnp.sum(share, axis=1, keepdims=True)
     label = jnp.where((lane >= 16) & (lane < 48), lane & 15, -1)
@@ -368,7 +394,8 @@
     meta = jnp.where((rows8 >> 2) == k, jnp.concatenate([table, table], axis=0), 0.0)
     high = meta.astype(BF16).astype(F32)
     meta = jnp.where(lane < 32, high, meta - high)
-    state = rs_last(0, rs_second(0)).astype(BF16)
+    halves = [rs_second(0, g) for g in range(GROUPS)]
+    state = jnp.concatenate([rs_last(0, g, halves[g]) for g in range(GROUPS)], axis=1).astype(BF16)
     state_wide = state.astype(F32)
     square = jnp.sum(state_wide * state_wide, axis=1, keepdims=True)
     top = square.astype(BF16).astype(F32)
@@ -378,56 +405,44 @@
     info = jnp.where(lane == 2, square - top - mid, info)
     xb[0, k, me, :, 0:HC] = state
     xb[0, k, me, :, HC:MSG] = info.astype(BF16)
-    cross = remote(xb.at[0, k, me], xb.at[1, k, me], z_s.at[0], z_r.at[0], far)
+    hello(2)
     go(cross)
     ag_start(0)
     for cp in loads[4:]:
         cp.wait()
-    begin = t
-
-    def enter():
-        cross.wait_recv()
-        ag_start(1)
-
-    def second():
-        ag_forward(0)
-        ag_pair(0)
-
-    when(t == 1)(enter)
+    when(late)(enter)
     ag_forward(begin)
     ag_pair(begin)
-    when(t == 1)(second)
     hidden = ffn(begin)
-    rs_pair_fill(1, hidden, wd)
-    rs_pair_go(1)
-    rs_own(hidden, wd)
-    when(t == 0)(enter)
-    rs_first(1)
-    when(t == 0)(functools.partial(ag_forward, 1))
-    v = rs_second(1)
-    when(t == 0)(functools.partial(ag_pair, 1))
-    v = rs_last(1, v)
+    rs_pair_send(1, hidden, wd)
+    for g in range(GROUPS):
+        rs_first(1, g, hidden, wd)
+    when(early)(enter)
+    halves = [rs_second(1, g) for g in range(GROUPS)]
+    ag_forward(1 - begin)
+    v = jnp.concatenate([rs_last(1, g, halves[g]) for g in range(GROUPS)], axis=1)
     first_moe[...] = v
     back = remote(xs, xr, z_s.at[1], z_r.at[1], far)
 
-    @when(t == 1)
+    @when(late)
     def _():
         xs[...] = v.astype(BF16)
         back.start()
 
+    ag_pair(1 - begin)
     hidden = ffn(1 - begin)
-    rs_pair_fill(2, hidden, wd)
-    rs_pair_go(2)
-    rs_own(hidden, wd)
-    rs_first(2)
-    last = rs_last(2, rs_second(2))
-
-    @when(t == 0)
+    rs_pair_send(2, hidden, wd)
+    for g in range(GROUPS):
+        rs_first(2, g, hidden, wd)
+    halves = [rs_second(2, g) for g in range(GROUPS)]
+    last = jnp.concatenate([rs_last(2, g, halves[g]) for g in range(GROUPS)], axis=1)
+
+    @when(early)
     def _():
         xs[...] = last.astype(BF16)
         back.start()
 
-    moe = jnp.where(t == 0, first_moe[...], last)
+    moe = jnp.where(early, first_moe[...], last)
     back.wait_recv()
     total = (state_wide + moe + xr[...].astype(F32)).astype(BF16).astype(F32)
     low, upper = total[0:4], total[4:8]
@@ -475,14 +490,14 @@
             VMEM((256, WIDE), BF16), VMEM((FF, WIDE), BF16), VMEM((FF, WIDE), BF16), VMEM((FF, WIDE), BF16),
             VMEM((2, 2, 16, 8, MSG), BF16), VMEM((16, 8, HC), F32), VMEM((4, 8, HC), F32),
             VMEM((3, 16, 8, HC), BF16), VMEM((3, 16, 8, HC), BF16),
-            VMEM((3, 3, 4, 8, HC), BF16), VMEM((3, 3, 4, 8, HC), BF16),
-            VMEM((3, 3, 8, HC), BF16), VMEM((3, 3, 8, HC), BF16),
+            VMEM((3, GROUPS, 3, 4, 8, GC), BF16), VMEM((3, GROUPS, 3, 4, 8, GC), BF16),
+            VMEM((3, GROUPS, 3, 8, GC), BF16), VMEM((3, GROUPS, 3, 8, GC), BF16),
             VMEM((8, HC), BF16), VMEM((8, HC), BF16), VMEM((4, HC), BF16), VMEM((4, HC), BF16),
             VMEM((8, HC), F32),
             dma((7,)), pltpu.SemaphoreType.REGULAR((3,)), pltpu.SemaphoreType.REGULAR((3,)),
             dma((8,)), dma((8,)), dma((7,)), dma((7,)), dma((15,)), dma((15,)), dma((15,)), dma((15,)),
             dma((2, 3)), dma((2, 3)), dma((2, 4, 3)), dma((2, 4, 3)), dma((2, 4, 4)), dma((2, 4, 4)),
-            dma((3, 3)), dma((3, 3)), dma((3, 3)), dma((3, 3)), dma((3, PARTS)), dma((3, PARTS)),
+            dma((3, GROUPS, 3)), dma((3, GROUPS, 3)), dma((3, GROUPS, 3)), dma((3, GROUPS, 3)), dma((3, PARTS)), dma((3, PARTS)),
             dma((2,)), dma((2,)), dma, dma,
         ],
         compiler_params=pltpu.CompilerParams(collective_id=0, has_side_effects=True),

time: 96.9 us -> 92.8 us (0.958)
  Pallas kernels: 95 us -> 91.2 us
    pallas_call x1, Pallas kernels: 95 us -> 91.2 us  [layer(): pl.pallas_call(layer_kernel, out_shape=jax.ShapeDtypeStruct((4, WIDE), BF...]
where the time goes in v4:
time: 92.8 us; the launch traced here: 92.6 us
  Pallas kernels  91.2 us (98%)
  local copies, waits for them, and re-layouts  1.39 us (1%)
    pallas_call x1, Pallas kernels, layer(): pl.pallas_call(layer_kernel, out_shape=jax.ShapeDtypeStruct((4, WIDE), BF...  91.2 us

profile of v4, /device:TPU:1, one launch (start us, length us, event | category | flops | bytes accessed | tf_op | source)
XLA Modules:
  0.0 92.6 jit_solution(8493987782921500306)
XLA Ops:
  0.0 91.2 %layer.1 = bf16[4,4096]{1,0:T(4,128)(2,1)} custom-call(s32[4,8]{1,0:T(4,128)} %routes_ref.1, f32[4,8]{1,0:T(4,128)} %weight_ref.1, f32[1,4096]{1,0:T(1,128)} %bitcast.11, bf16[256,128]{1,0:T(8,128)(2,1)} %bitcast.10, bf16[1024,128]{1,0:T(8,128)(2,1)} %bitcast.8, bf16[1024,128]{1,0:T(8,128)(2,1)} %bitcast.9, bf16[256,4096]{1,0:T(8,128)(2,1)} %wo_hbm.1, ...), custom_call_target="tpu_custom_call" | custom-call | tf_op jit(solution)/shard_map/layer/pallas_call | solution.py:481
  91.2 1.4 %copy.12 = bf16[4,4096]{1,0:T(4,128)(2,1)} copy(bf16[4,4096]{1,0:T(4,128)(2,1)} %layer.1) | data formatting | bytes 65536
